TPU v7x, 32 devices: a whole 2x2x4 slice. The times are simulated.
32 devices in a mesh: dp: 8 (over y, x, core), tensor: 4 (over z).
Axes of the slice: x: 2, y: 2, z: 4, core: 2. Of those that a mesh axis runs over, the one named last changes fastest.
Arguments:
- x_in: bfloat16 [16384, 768], P(('dp', 'tensor')), may hold values from -6 to 6
- bucket: int32 [32], P(('dp', 'tensor')), may hold values from 0 to 1
- lengths: int32 [32, 4], P(('dp', 'tensor')), may hold values from 32 to 128, as said below
- qkv_weight: bfloat16 [2, 768, 2304], replicated, may hold values from -0.21875 to 0.21875
- out_weight: bfloat16 [2, 768, 768], replicated, may hold values from -0.875 to 0.875
- norm_gain1: float32 [2, 768], replicated, may hold values from 0.5 to 1.5
- norm_bias1: float32 [2, 768], replicated, may hold values from -1.8 to 1.8
- up_weight: bfloat16 [2, 768, 2, 3072], P(None, None, None, 'tensor'), may hold values from -0.21875 to 0.21875
- down_weight: bfloat16 [2, 3072, 768], P(None, 'tensor'), may hold values from -0.109375 to 0.109375
- norm_gain2: float32 [2, 768], replicated, may hold values from 0.5 to 1.5
- norm_bias2: float32 [2, 768], replicated, may hold values from -1.8 to 1.8
- cotangent: bfloat16 [16384, 768], P(('dp', 'tensor')), may hold values from -6 to 6
Outputs:
- activations: bfloat16 [2, 16384, 768], P(None, ('dp', 'tensor'))
- input_grad: float32 [16384, 768], P(('dp', 'tensor'))
- qkv_grad: float32 [2, 768, 2304], replicated
- out_grad: float32 [2, 768, 768], replicated
- gain1_grad: float32 [2, 768], replicated
- bias1_grad: float32 [2, 768], replicated
- up_grad: float32 [2, 768, 2, 3072], P(None, 'dp', None, 'tensor')
- down_grad: float32 [2, 3072, 768], P(None, 'tensor', 'dp')
- gain2_grad: float32 [2, 768], replicated
- bias2_grad: float32 [2, 768], replicated
Inputs may be any that keep to these rules, and one draw needn't show every extreme that they name: Every entry is a length of a short sequence; each row of lengths has an entry equal to 128. A block of bucket 1 holds one sequence whose length is the sum of its row of lengths.
All inputs are finite; a program needn't handle non-finite values.
Results may differ from a plain program's by a relative error of at most 0.033.
Values may be sent and summed in bfloat16 or wider, within the bound.
No kernel may reach another device: no remote copies, remote signals or barrier semaphores. Data moves between devices by JAX's collectives and lax.ppermute only.
A program may use at most 256 MiB of HBM per device.

v0:
```python
import jax
import jax.numpy as jnp
from jax import lax
from jax.sharding import PartitionSpec as P

HEADS = 12
HEAD_DIM = 64
SHORT = 128
LAYERS = 2
eps_norm = 1e-05
gelu_coef = 0.7978845608028654
masked_score = -1e30


def segments(bucket_one, lens, rows_dev, short_len):
    rows = jnp.arange(rows_dev, dtype=jnp.int32)
    slot = rows // short_len
    offset = rows - slot * short_len
    slots_all = jnp.arange(lens.shape[0], dtype=jnp.int32)
    slot_len = jnp.sum(jnp.where(slot[:, None] == slots_all[None, :], lens[None, :], 0), axis=1)
    total = jnp.sum(lens)
    is_long = bucket_one == 1
    real = jnp.where(is_long, rows < total, offset < slot_len)
    group = jnp.where(is_long, 0, slot)
    return jnp.where(real, group, lens.shape[0] + rows)


def alibi(rows_dev, heads):
    slopes = jnp.exp2(-8.0 * (jnp.arange(heads, dtype=jnp.float32) + 1.0) / heads)
    place = jnp.arange(rows_dev, dtype=jnp.float32)
    dist = jnp.abs(place[:, None] - place[None, :])
    return slopes[:, None, None] * dist[None, :, :]


def layer_norm(value, gain, bias):
    mean = jnp.mean(value, axis=-1, keepdims=True)
    centered = value - mean
    var = jnp.mean(centered * centered, axis=-1, keepdims=True)
    return centered * lax.rsqrt(var + eps_norm) * gain + bias


def geglu(joined):
    half = joined.shape[1] // 2
    gate = joined[:, :half]
    value = joined[:, half:]
    return 0.5 * gate * (1.0 + jnp.tanh(gelu_coef * (gate + 0.044715 * gate * gate * gate))) * value


def split_heads(qkv_low, width):
    rows = qkv_low.shape[0]
    query = qkv_low[:, :width].reshape(rows, HEADS, HEAD_DIM)
    keys = qkv_low[:, width : 2 * width].reshape(rows, HEADS, HEAD_DIM)
    values = qkv_low[:, 2 * width :].reshape(rows, HEADS, HEAD_DIM)
    return (query, keys, values)


def scores_of(query, keys, same, decay):
    raw = (
        jnp.einsum("qhe,khe->hqk", query, keys, preferred_element_type=jnp.float32)
        * HEAD_DIM ** (-0.5)
        - decay
    )
    return jnp.where(same[None, :, :], raw, masked_score)


def forward_layer(x_low, wqkv, wo, g1, b1, wup, wdown, g2, b2, same, decay):
    rows = x_low.shape[0]
    width = x_low.shape[1]
    qkv_low = jnp.dot(x_low, wqkv, preferred_element_type=jnp.float32).astype(jnp.bfloat16)
    query, keys, values = split_heads(qkv_low, width)
    scores = scores_of(query, keys, same, decay)
    top = jnp.max(scores, axis=-1, keepdims=True)
    log_total = top + jnp.log(jnp.sum(jnp.exp(scores - top), axis=-1, keepdims=True))
    probs_low = jnp.exp(scores - log_total).astype(jnp.bfloat16)
    ctx_low = (
        jnp.einsum("hqk,khe->qhe", probs_low, values, preferred_element_type=jnp.float32)
        .reshape(rows, width)
        .astype(jnp.bfloat16)
    )
    attn = jnp.dot(ctx_low, wo, preferred_element_type=jnp.float32)
    pre_first = x_low.astype(jnp.float32) + attn
    normed = layer_norm(pre_first, g1, b1)
    normed_low = normed.astype(jnp.bfloat16)
    gathered = lax.all_gather(normed_low, "tensor", axis=0, tiled=True)
    joined = jnp.dot(gathered, wup.reshape(width, -1), preferred_element_type=jnp.float32)
    act_low = geglu(joined).astype(jnp.bfloat16)
    mixed = lax.psum_scatter(
        jnp.dot(act_low, wdown, preferred_element_type=jnp.float32).astype(jnp.bfloat16),
        "tensor",
        scatter_dimension=0,
        tiled=True,
    ).astype(jnp.float32)
    pre_second = normed + mixed
    out_low = layer_norm(pre_second, g2, b2).astype(jnp.bfloat16)
    keep = (
        x_low,
        qkv_low,
        log_total,
        ctx_low,
        pre_first,
        normed_low,
        pre_second,
        gathered,
        joined,
        act_low,
    )
    return (out_low, keep)


def backward_layer(grad_out, keep, wqkv, wo, g1, b1, wup, wdown, g2, b2, same, decay):
    (
        x_low,
        qkv_low,
        log_total,
        ctx_low,
        pre_first,
        normed_low,
        pre_second,
        gathered,
        joined,
        act_low,
    ) = keep
    rows = x_low.shape[0]
    width = x_low.shape[1]
    up_flat = wup.reshape(width, -1)
    second_pull = jax.vjp(layer_norm, pre_second, g2, b2)[1]
    d_pre2, d_gain2, d_bias2 = second_pull(grad_out)
    grad_rows = lax.all_gather(d_pre2.astype(jnp.bfloat16), "tensor", axis=0, tiled=True)
    d_act = jnp.dot(grad_rows, wdown.T, preferred_element_type=jnp.float32)
    d_down = jnp.dot(act_low.T, grad_rows, preferred_element_type=jnp.float32)
    geglu_pull = jax.vjp(geglu, joined)[1]
    d_joined = geglu_pull(d_act)[0].astype(jnp.bfloat16)
    d_up = jnp.dot(gathered.T, d_joined, preferred_element_type=jnp.float32).reshape(wup.shape)
    d_normed = d_pre2 + lax.psum_scatter(
        jnp.dot(d_joined, up_flat.T, preferred_element_type=jnp.float32).astype(jnp.bfloat16),
        "tensor",
        scatter_dimension=0,
        tiled=True,
    ).astype(jnp.float32)
    first_pull = jax.vjp(layer_norm, pre_first, g1, b1)[1]
    d_pre1, d_gain1, d_bias1 = first_pull(d_normed)
    d_attn_low = d_pre1.astype(jnp.bfloat16)
    d_wo = jnp.dot(ctx_low.T, d_attn_low, preferred_element_type=jnp.float32)
    d_ctx = (
        jnp.dot(d_attn_low, wo.T, preferred_element_type=jnp.float32)
        .astype(jnp.bfloat16)
        .reshape(rows, HEADS, HEAD_DIM)
    )
    query, keys, values = split_heads(qkv_low, width)
    probs = jnp.exp(scores_of(query, keys, same, decay) - log_total)
    probs_low = probs.astype(jnp.bfloat16)
    d_values = jnp.einsum("hqk,qhe->khe", probs_low, d_ctx, preferred_element_type=jnp.float32)
    d_probs = jnp.einsum("qhe,khe->hqk", d_ctx, values, preferred_element_type=jnp.float32)
    d_scores = (probs * (d_probs - jnp.sum(probs * d_probs, axis=-1, keepdims=True))).astype(
        jnp.bfloat16
    )
    d_query = jnp.einsum(
        "hqk,khe->qhe", d_scores, keys, preferred_element_type=jnp.float32
    ) * HEAD_DIM ** (-0.5)
    d_keys = jnp.einsum(
        "hqk,qhe->khe", d_scores, query, preferred_element_type=jnp.float32
    ) * HEAD_DIM ** (-0.5)
    d_qkv = jnp.concatenate(
        [d_query.reshape(rows, width), d_keys.reshape(rows, width), d_values.reshape(rows, width)],
        axis=1,
    ).astype(jnp.bfloat16)
    d_wqkv = jnp.dot(x_low.T, d_qkv, preferred_element_type=jnp.float32)
    d_input = d_pre1 + jnp.dot(d_qkv, wqkv.T, preferred_element_type=jnp.float32)
    return (d_input, d_wqkv, d_wo, d_gain1, d_bias1, d_up, d_down, d_gain2, d_bias2)


def shards(
    x_in,
    bucket,
    lengths,
    qkv_weight,
    out_weight,
    norm_gain1,
    norm_bias1,
    up_weight,
    down_weight,
    norm_gain2,
    norm_bias2,
    cotangent,
):
    rows = x_in.shape[0]
    seg = segments(bucket[0], lengths[0], rows, SHORT)
    same = seg[:, None] == seg[None, :]
    decay = alibi(rows, HEADS)
    layer_in = x_in
    outputs = []
    kept = []
    for layer in range(LAYERS):
        layer_in, keep = forward_layer(
            layer_in,
            qkv_weight[layer],
            out_weight[layer],
            norm_gain1[layer],
            norm_bias1[layer],
            up_weight[layer],
            down_weight[layer],
            norm_gain2[layer],
            norm_bias2[layer],
            same,
            decay,
        )
        outputs.append(layer_in)
        kept.append(keep)
    grad = cotangent.astype(jnp.float32)
    found = [None] * LAYERS
    for layer in reversed(range(LAYERS)):
        grad, d_wqkv, d_wo, d_gain1, d_bias1, d_up, d_down, d_gain2, d_bias2 = backward_layer(
            grad,
            kept[layer],
            qkv_weight[layer],
            out_weight[layer],
            norm_gain1[layer],
            norm_bias1[layer],
            up_weight[layer],
            down_weight[layer],
            norm_gain2[layer],
            norm_bias2[layer],
            same,
            decay,
        )
        d_wqkv, d_wo, d_gain1, d_bias1, d_gain2, d_bias2 = lax.psum(
            (d_wqkv, d_wo, d_gain1, d_bias1, d_gain2, d_bias2), ("dp", "tensor")
        )
        d_up, d_down = (
            lax.psum_scatter(
                d_up.astype(jnp.bfloat16), "dp", scatter_dimension=0, tiled=True
            ).astype(jnp.float32),
            lax.psum_scatter(
                d_down.astype(jnp.bfloat16), "dp", scatter_dimension=1, tiled=True
            ).astype(jnp.float32),
        )
        found[layer] = (d_wqkv, d_wo, d_gain1, d_bias1, d_up, d_down, d_gain2, d_bias2)
    stacked = [jnp.stack([found[layer][index] for layer in range(LAYERS)]) for index in range(8)]
    qkv_grad, out_grad, gain1_grad, bias1_grad, up_grad, down_grad, gain2_grad, bias2_grad = stacked
    activations = jnp.stack(outputs)
    return (
        activations,
        grad,
        qkv_grad,
        out_grad,
        gain1_grad,
        bias1_grad,
        up_grad,
        down_grad,
        gain2_grad,
        bias2_grad,
    )


def solution(mesh):
    in_specs = (
        P(("dp", "tensor"), None),
        P(("dp", "tensor")),
        P(("dp", "tensor"), None),
        P(),
        P(),
        P(),
        P(),
        P(None, None, None, "tensor"),
        P(None, "tensor", None),
        P(),
        P(),
        P(("dp", "tensor"), None),
    )
    out_specs = (
        P(None, ("dp", "tensor"), None),
        P(("dp", "tensor"), None),
        P(),
        P(),
        P(),
        P(),
        P(None, "dp", None, "tensor"),
        P(None, "tensor", "dp"),
        P(),
        P(),
    )
    return jax.shard_map(shards, mesh=mesh, in_specs=in_specs, out_specs=out_specs, check_vma=False)
```

profile of v0, /device:TPU:0, one launch (start us, length us, event | category | flops | bytes accessed | tf_op | source)
XLA Modules:
  0.0 1206.9 jit_solution(10613801410674038543)
XLA Ops:
  12.0 4.2 convolution_convert_fusion.1
  17.3 5.0 fusion.103
  32.5 7.0 fusion.100
  41.4 57.2 %all-gather.5.cloned.1.call-done = bf16[2048,768]{1,0:T(8,128)(2,1)} async-done(((bf16[512,768]{1,0:T(8,128)(2,1)}), bf16[2048,768]{1,0:T(8,128)(2,1)}) %all-gather.5.cloned.1.call-update) | async-done | bytes 3145744 | tf_op jit(solution)/shard_map/all_gather | solution.py:84
  98.6 7.7 fusion.107
  108.6 2.8 copy-done.8
  113.1 3.9 convolution_convert_fusion.5
  117.8 58.3 %reduce-scatter.7.cloned.1.call-done = bf16[512,768]{1,0:T(8,128)(2,1)} async-done(((bf16[2048,768]{1,0:T(8,128)(2,1)}), bf16[512,768]{1,0:T(8,128)(2,1)}) %reduce-scatter.7.cloned.1.call-update) | async-done | bytes 786448 | tf_op jit(solution)/shard_map/reduce_scatter | solution.py:87
  178.1 4.1 convolution_convert_fusion
  187.6 4.9 fusion.105
  201.9 3.5 copy.112
  205.4 60.0 %all-gather.7.cloned.1.call-done = bf16[2048,768]{1,0:T(8,128)(2,1)} async-done(((bf16[512,768]{1,0:T(8,128)(2,1)}), bf16[2048,768]{1,0:T(8,128)(2,1)}) %all-gather.7.cloned.1.call-update) | async-done | bytes 3145744 | tf_op jit(solution)/shard_map/all_gather | solution.py:84
  265.3 7.7 fusion.108
  275.3 2.8 copy-done.9
  279.7 3.9 convolution_convert_fusion.4
  283.7 59.0 %reduce-scatter.9.cloned.1.call-done = bf16[512,768]{1,0:T(8,128)(2,1)} async-done(((bf16[2048,768]{1,0:T(8,128)(2,1)}), bf16[512,768]{1,0:T(8,128)(2,1)}) %reduce-scatter.9.cloned.1.call-update) | async-done | bytes 786448 | tf_op jit(solution)/shard_map/reduce_scatter | solution.py:87
  350.1 63.4 %all-gather.9.cloned.1.call-done = bf16[2048,768]{1,0:T(8,128)(2,1)} async-done(((bf16[512,768]{1,0:T(8,128)(2,1)}), bf16[2048,768]{1,0:T(8,128)(2,1)}) %all-gather.9.cloned.1.call-update) | async-done | bytes 3145744 | tf_op jit(solution)/shard_map/all_gather | solution.py:128
  413.6 12.0 fusion.25
  430.2 6.4 convolution_convert_fusion.7
  436.7 59.0 %reduce-scatter.11.cloned.1.call-done = bf16[512,768]{1,0:T(8,128)(2,1)} async-done(((bf16[2048,768]{1,0:T(8,128)(2,1)}), bf16[512,768]{1,0:T(8,128)(2,1)}) %reduce-scatter.11.cloned.1.call-update) | async-done | bytes 786448 | tf_op jit(solution)/shard_map/reduce_scatter | solution.py:134
  495.7 3.2 multiply_reduce_fusion.3
  502.1 7.7 fusion.51
  509.8 9.2 multiply_reduce_fusion.1
  519.0 6.9 multiply_convert_fusion.1
  536.6 63.6 %all-gather.11.cloned.1.call-done = bf16[2048,768]{1,0:T(8,128)(2,1)} async-done(((bf16[512,768]{1,0:T(8,128)(2,1)}), bf16[2048,768]{1,0:T(8,128)(2,1)}) %all-gather.11.cloned.1.call-update) | async-done | bytes 3145744 | tf_op jit(solution)/shard_map/all_gather | solution.py:128
  600.3 12.6 %fusion.24 = (f32[2048,768]{1,0:T(8,128)S(1)}, f32[2048,768]{1,0:T(8,128)S(1)}) fusion(f32[2048,1536]{1,0:T(8,128)} %copy-done.8, bf16[2048,768]{1,0:T(8,128)(2,1)} %all-gather.11.cloned.1.call-done, bf16[2,768,768]{2,1,0:T(8,128)(2,1)} %param.20), kind=kOutput, calls=%fused_computation.69 | convolution fusion | flops 2456813568 | bytes 29491200 | tf_op jit(solution)/shard_map/dot_general | solution.py:129
  612.8 2.7 copy-done.81
  617.6 6.4 convolution_convert_fusion.6
  624.1 6.5 convolution_convert_fusion.8
  630.9 12.0 convolution_convert_fusion.2
  642.9 6.0 convert_element_type.181
  648.9 6.6 convolution_convert_fusion.9
  655.8 3.6 convolution_bitcast_fusion.2
  659.4 5.0 convolution_bitcast_fusion
  664.5 9.3 convolution_convert_fusion.3
  673.7 6.0 convert_element_type.179
  679.8 3.3 reduce-scatter.13.cloned.1.call-done
  691.0 10.9 multiply_reduce_fusion
  704.0 7.0 multiply_convert_fusion
  719.5 5.0 convolution_bitcast_fusion.1
  728.1 35.8 %reduce-scatter.15.cloned.1.call-done = bf16[768,96]{0,1:T(8,128)(2,1)} async-done(((bf16[768,768]{0,1:T(8,128)(2,1)}), bf16[768,96]{0,1:T(8,128)(2,1)}) %reduce-scatter.15.cloned.1.call-update) | async-done | bytes 147472 | tf_op jit(solution)/shard_map/reduce_scatter | solution.py:233
  765.8 88.5 %all-reduce.14.cloned.1.call-done = (bf16[768,2,768]{2,1,0:T(2,128)(2,1)}, bf16[768,2,768]{2,1,0:T(2,128)(2,1)}) async-done(((bf16[768,2,768]{2,1,0:T(2,128)(2,1)}, bf16[768,2,768]{2,1,0:T(2,128)(2,1)}), (bf16[768,2,768]{2,1,0:T(2,128)(2,1)}, bf16[768,2,768]{2,1,0:T(2,128)(2,1)})) %all-reduce.14.cloned.1.call-update) | async-done | bytes 4718608
  858.5 41.8 %all-reduce.6 = (f32[1,768]{1,0:T(1,128)S(1)}, f32[1,768]{1,0:T(1,128)S(1)}, f32[1,768]{1,0:T(1,128)S(1)}, f32[1,768]{1,0:T(1,128)S(1)}, f32[1,768]{1,0:T(1,128)...) all-reduce(f32[1,768]{1,0:T(1,128)S(1)} %stack.101, ...), channel_id=1, replica_groups=mesh['dp'=8,'tensor'=4] {'dp','tensor'}, use_global_device_ids=true, to_apply=%region_35.36 | all-reduce | flops 6144 | bytes 49152 | tf_op jit(solution)/shard_map/psum | solution.py:226
  902.7 5.5 add_add_fusion.4
  908.2 260.8 %all-reduce.12.cloned.1.call-done = (f32[1,768,2304]{1,2,0:T(8,128)}, f32[1,768,2304]{1,2,0:T(8,128)}, f32[1,768,768]{2,1,0:T(8,128)}, f32[1,768,768]{2,1,0:T(8,128)}) async-done(((f32[1,768,2304]{1,2,0:T(8,128)}, f32[1,768,2304]{1,2,0:T(8,128)}, f32[1,768,768]{2,1,0:T(8,128)}, f32[1,768,768]{2,1,0:T(8,128)}), (f32[1,768,2304]{1,2,0:T(8,128)}, f32[1,768,2304]{1,2,0:T(8,128)}, f32[1,768,768]{2,1,0:T(8,128)}, ...) | async-done | bytes 18874384 | tf_op jit(solution)/shard_map/psum | solution.py:226
  1169.0 11.0 pad_maximum_fusion
  1179.9 15.4 %copy.101 = f32[2,768,2304]{2,1,0:T(8,128)} copy(f32[2,768,2304]{1,2,0:T(8,128)} %pad_maximum_fusion) | data formatting | bytes 28311552
  1195.4 4.2 pad_maximum_fusion.1
  (302 shorter events, 100.0 us)
Async XLA Ops:
  7.2 91.5 %all-gather.5.cloned.1.call-start = ((), (), s32[]{:S(2)}) async-start(), calls=%async_computation.6 | async-start | bytes 3932160 | tf_op jit(solution)/shard_map/all_gather | solution.py:84
  16.7 5.7 copy-start.14
  17.0 5.4 copy-start.32
  17.3 7.0 copy-start.10
  24.3 4.7 copy-start.42
  29.9 146.2 %copy-start.2 = (f32[512,768]{1,0:T(8,128)}, f32[512,768]{1,0:T(8,128)S(1)}, u32[]{:S(2)}) copy-start(f32[512,768]{1,0:T(8,128)S(1)} %get-tuple-element.112) | copy-start | bytes 4718596
  30.0 146.2 %copy-start.53 = (f32[512]{0:T(512)}, f32[512]{0:T(512)S(1)}, u32[]{:S(2)}) copy-start(f32[512]{0:T(512)S(1)} %broadcast_multiply_fusion.3) | copy-start | bytes 6148
  31.0 145.1 %copy-start.55 = (f32[512]{0:T(512)}, f32[512]{0:T(512)S(1)}, u32[]{:S(2)}) copy-start(f32[512]{0:T(512)S(1)} %fusion.80) | copy-start | bytes 6148
  31.1 145.1 %copy-start.51 = (f32[768]{0:T(1024)}, f32[768]{0:T(1024)S(1)}, u32[]{:S(2)}) copy-start(f32[768]{0:T(1024)S(1)} %get-tuple-element.122) | copy-start | bytes 9220
  32.3 143.8 %reduce-scatter.7.cloned.1.call-start = ((), (), s32[]{:S(2)}) async-start(), calls=%async_computation.7 | async-start | bytes 3932160 | tf_op jit(solution)/shard_map/reduce_scatter | solution.py:87
  106.4 5.0 copy-start.8
  106.4 6.7 copy-start.70
  117.0 148.3 %all-gather.7.cloned.1.call-start = ((), (), s32[]{:S(2)}) async-start(), calls=%async_computation.8 | async-start | bytes 3932160 | tf_op jit(solution)/shard_map/all_gather | solution.py:84
  117.8 81.4 %copy-start.59 = (f32[768]{0:T(1024)}, f32[768]{0:T(1024)S(1)}, u32[]{:S(2)}) copy-start(f32[768]{0:T(1024)S(1)} %get-tuple-element.65) | copy-start | bytes 9220
  185.0 7.6 copy-start.16
  187.6 6.9 copy-start.12
  201.7 141.1 %reduce-scatter.9.cloned.1.call-start = ((), (), s32[]{:S(2)}) async-start(), calls=%async_computation.9 | async-start | bytes 3932160 | tf_op jit(solution)/shard_map/reduce_scatter | solution.py:87
  273.1 5.0 copy-start.9
  273.1 6.6 copy-start.71
  283.7 129.9 %all-gather.9.cloned.1.call-start = ((), (), s32[]{:S(2)}) async-start(), calls=%async_computation.10 | async-start | bytes 3932160 | tf_op jit(solution)/shard_map/all_gather | solution.py:128
  349.9 145.8 %reduce-scatter.11.cloned.1.call-start = ((), (), s32[]{:S(2)}) async-start(), calls=%async_computation.11 | async-start | bytes 3932160 | tf_op jit(solution)/shard_map/reduce_scatter | solution.py:134
  413.6 16.6 %copy-start.40 = (bf16[96,8,2,768]{3,1,2,0:T(8,128)(2,1)S(1)}, bf16[96,8,2,768]{3,1,2,0:T(8,128)(2,1)}, u32[]{:S(2)}) copy-start(bf16[96,8,2,768]{3,1,2,0:T(8,128)(2,1)} %copy.112) | copy-start | bytes 7077892
  436.6 163.6 %all-gather.11.cloned.1.call-start = ((), (), s32[]{:S(2)}) async-start(), calls=%async_computation.12 | async-start | bytes 3932160 | tf_op jit(solution)/shard_map/all_gather | solution.py:128
  502.1 7.7 copy-start.13
  502.1 16.9 %slice-start.3 = ((s8[12582912]{0:T(1024)(128)(4,1)}), s8[4194304]{0:T(1024)(128)(4,1)S(1)}, s32[]{:S(2)}) async-start(s8[12582912]{0:T(1024)(128)(4,1)} %bitcast.151), calls=%async_computation.21 | async-start | bytes 8388608
  502.1 16.9 %slice-start.4 = ((s8[12582912]{0:T(1024)(128)(4,1)}), s8[4194304]{0:T(1024)(128)(4,1)S(1)}, s32[]{:S(2)}) async-start(s8[12582912]{0:T(1024)(128)(4,1)} %bitcast.151), calls=%async_computation.22 | async-start | bytes 8388608
  509.8 9.2 slice-start.5
  519.0 6.9 copy-start.34
  536.6 146.5 %reduce-scatter.13.cloned.1.call-start = ((), (), s32[]{:S(2)}) async-start(), calls=%async_computation.13 | async-start | bytes 3932160 | tf_op jit(solution)/shard_map/reduce_scatter | solution.py:134
  600.3 17.3 %copy-start.39 = (bf16[96,8,2,768]{3,1,2,0:T(8,128)(2,1)S(1)}, bf16[96,8,2,768]{3,1,2,0:T(8,128)(2,1)}, u32[]{:S(2)}) copy-start(bf16[96,8,2,768]{3,1,2,0:T(8,128)(2,1)} %copy.111) | copy-start | bytes 7077892
  612.8 4.8 copy-start.82
  624.0 104.1 %reduce-scatter.17.cloned.1.call-start = ((), (), s32[]{:S(2)}) async-start(), calls=%async_computation.15 | async-start | bytes 1327104 | tf_op jit(solution)/shard_map/reduce_scatter | solution.py:233
  630.6 133.3 %reduce-scatter.15.cloned.1.call-start = ((), (), s32[]{:S(2)}) async-start(), calls=%async_computation.14 | async-start | bytes 1327104 | tf_op jit(solution)/shard_map/reduce_scatter | solution.py:233
  655.5 198.8 %all-reduce.14.cloned.1.call-start = ((), (), s32[]{:S(2)}) async-start(), calls=%async_computation.17 | async-start | bytes 9437184
  655.8 8.6 slice-start.8
  659.4 5.0 copy-start.69
  659.4 5.0 slice-start.9
  679.8 6.0 copy-start.58
  679.8 489.2 %all-reduce.12.cloned.1.call-start = ((), (), s32[]{:S(2)}) async-start(), calls=%async_computation.16 | async-start | bytes 37748736 | tf_op jit(solution)/shard_map/psum | solution.py:226
  690.9 11.0 slice-start
  691.0 11.6 slice-start.1
  691.0 13.0 %slice-start.2 = ((s8[12582912]{0:T(1024)(128)(4,1)}), s8[4194304]{0:T(1024)(128)(4,1)S(1)}, s32[]{:S(2)}) async-start(s8[12582912]{0:T(1024)(128)(4,1)} %bitcast.149), calls=%async_computation.20 | async-start | bytes 8388608
  704.0 7.0 copy-start.19
  704.0 7.0 copy-start.26
  728.0 174.6 %copy-start.20 = (f32[512,768]{1,0:T(8,128)S(1)}, f32[512,768]{1,0:T(8,128)}, u32[]{:S(2)}) copy-start(f32[512,768]{1,0:T(8,128)} %copy-done.18) | copy-start | bytes 4718596
  728.0 174.6 %copy-start.36 = (bf16[12,64,512]{2,1,0:T(8,128)(2,1)S(1)}, bf16[12,64,512]{2,1,0:T(8,128)(2,1)}, u32[]{:S(2)}) copy-start(bf16[12,64,512]{2,1,0:T(8,128)(2,1)} %copy-done.35) | copy-start | bytes 2359300
  728.0 174.6 %copy-start.45 = (bf16[12,64,512]{2,1,0:T(8,128)(2,1)S(1)}, bf16[12,64,512]{2,1,0:T(8,128)(2,1)}, u32[]{:S(2)}) copy-start(bf16[12,64,512]{2,1,0:T(8,128)(2,1)} %copy-done.44) | copy-start | bytes 2359300
  1179.9 15.4 %copy-start.41 = (f32[1,768,768]{2,1,0:T(8,128)S(1)}, f32[1,768,768]{2,1,0:T(8,128)}, u32[]{:S(2)}) copy-start(f32[1,768,768]{2,1,0:T(8,128)} %get-tuple-element.80) | copy-start | bytes 7077892
  (57 other events, 135.6 us)
Sparse Core Ops, SparseCore 0:
  32.4 66.1 all-gather.4
  117.2 58.8 reduce-scatter.6
  201.8 63.5 all-gather.6
  283.8 58.8 reduce-scatter.8
  350.0 63.5 all-gather.8
  436.7 58.8 reduce-scatter.10
  536.7 63.5 all-gather.10
  624.2 58.8 reduce-scatter.12
  686.9 36.8 reduce-scatter.16
  727.2 36.7 reduce-scatter.14
  767.3 86.9 all-reduce.13
  862.3 306.5 all-reduce.11
where the time goes:
time: 1220 us; the launch traced here: 1210 us
  waiting for transfers between devices  809 us (66%)
  matrix products  182 us (15%)
  local copies, waits for them, and re-layouts  85.4 us (7%)
  other arithmetic  69 us (6%)
  blocking collectives  41.8 us (3%)
  between operations  17.3 us (1%)
    psum x1, waiting for transfers between devices, shards(): lax.psum((d_wqkv, d_wo, d_gain1, d_bias1, d_gain2, d_bias2), ('dp', 'tens...  261 us
    all_gather x2, waiting for transfers between devices, backward_layer(): lax.all_gather(d_pre2.astype(jnp.bfloat16), 'tensor', axis=0, tiled=True)  127 us
    reduce_scatter x2, waiting for transfers between devices, forward_layer(): lax.psum_scatter(jnp.dot(act_low, wdown, preferred_element_type=jnp.float...  117 us
    all_gather x2, waiting for transfers between devices, forward_layer(): gathered = lax.all_gather(normed_low, 'tensor', axis=0, tiled=True)  117 us
    unnamed x13, waiting for transfers between devices  88.7 us
    reduce_scatter x2, waiting for transfers between devices, backward_layer(): lax.psum_scatter(jnp.dot(d_joined, up_flat.T, preferred_element_type=jnp....  62.3 us
    unnamed x190, local copies, waits for them, and re-layouts  56 us
    psum x1, blocking collectives, shards(): lax.psum((d_wqkv, d_wo, d_gain1, d_bias1, d_gain2, d_bias2), ('dp', 'tens...  41.8 us
  transfers between devices with their start and end apart: 12, of which 11 were waited for; matrix products, arithmetic and copies ran while one was open for 10% of the time, Pallas kernels for 0%

commit v1 on v0

--- a/solution.py
+++ b/solution.py
@@ -10,6 +10,27 @@
 eps_norm = 1e-05
 gelu_coef = 0.7978845608028654
 masked_score = -1e30
+
+
+def ring_gather(x, axis, dim):
+    size, index, rows = (lax.axis_size(axis), lax.axis_index(axis), x.shape[dim])
+    right = [(i, (i + 1) % size) for i in range(size)]
+    left = [(i, (i - 1) % size) for i in range(size)]
+    whole = jnp.zeros((*x.shape[:dim], size * rows, *x.shape[dim + 1 :]), x.dtype)
+    whole = lax.dynamic_update_slice_in_dim(whole, x, index * rows, axis=dim)
+    from_left = from_right = x
+    halfway = size // 2
+    for step in range(1, halfway + 1):
+        from_left = lax.ppermute(from_left, axis, right)
+        whole = lax.dynamic_update_slice_in_dim(
+            whole, from_left, (index - step) % size * rows, axis=dim
+        )
+        if step < size - halfway:
+            from_right = lax.ppermute(from_right, axis, left)
+            whole = lax.dynamic_update_slice_in_dim(
+                whole, from_right, (index + step) % size * rows, axis=dim
+            )
+    return whole
 
 
 def segments(bucket_one, lens, rows_dev, short_len):
@@ -125,7 +146,7 @@
     up_flat = wup.reshape(width, -1)
     second_pull = jax.vjp(layer_norm, pre_second, g2, b2)[1]
     d_pre2, d_gain2, d_bias2 = second_pull(grad_out)
-    grad_rows = lax.all_gather(d_pre2.astype(jnp.bfloat16), "tensor", axis=0, tiled=True)
+    grad_rows = ring_gather(d_pre2.astype(jnp.bfloat16), "tensor", 0)
     d_act = jnp.dot(grad_rows, wdown.T, preferred_element_type=jnp.float32)
     d_down = jnp.dot(act_low.T, grad_rows, preferred_element_type=jnp.float32)
     geglu_pull = jax.vjp(geglu, joined)[1]

time: 1220 us -> 1200 us (0.984)
  waiting for transfers between devices: 809 us -> 751 us
  starting transfers between devices: 1.89 us -> 37.5 us
    all_gather x2 -> x0, waiting for transfers between devices: 127 us -> none  [backward_layer(): lax.all_gather(d_pre2.astype(jnp.bfloat16), 'tensor', axis=0, tiled=True)]
    ppermute x0 -> x6, waiting for transfers between devices: none -> 69.3 us  [the longest x4 67.8 us: ring_gather(): from_left = lax.ppermute(from_left, axis, right)]
    ppermute x0 -> x6, starting transfers between devices: none -> 35.9 us  [the longest x4 30.2 us: ring_gather(): from_left = lax.ppermute(from_left, axis, right)]
    unnamed x190 -> x196, local copies, waits for them, and re-layouts: 56 us -> 51.6 us
    unnamed x13 -> x11, waiting for transfers between devices: 88.7 us -> 88.7 us
  transfers between devices with their start and end apart: 12 -> 16, of which waited for: 11 -> 14; matrix products, arithmetic and copies ran while one was open for 10% -> 11% of each run, Pallas kernels for 0% -> 0%
where the time goes in v1:
time: 1200 us; the launch traced here: 1190 us
  waiting for transfers between devices  751 us (63%)
  matrix products  185 us (15%)
  local copies, waits for them, and re-layouts  87.9 us (7%)
  other arithmetic  69.6 us (6%)
  blocking collectives  41.8 us (3%)
  starting transfers between devices  37.5 us (3%)
  between operations  17.3 us (1%)
    psum x1, waiting for transfers between devices, shards(): lax.psum((d_wqkv, d_wo, d_gain1, d_bias1, d_gain2, d_bias2), ('dp', 'tens...  261 us
    reduce_scatter x2, waiting for transfers between devices, forward_layer(): lax.psum_scatter(jnp.dot(act_low, wdown, preferred_element_type=jnp.float...  117 us
    all_gather x2, waiting for transfers between devices, forward_layer(): gathered = lax.all_gather(normed_low, 'tensor', axis=0, tiled=True)  117 us
    unnamed x11, waiting for transfers between devices  88.7 us
    ppermute x4, waiting for transfers between devices, ring_gather(): from_left = lax.ppermute(from_left, axis, right)  67.8 us
    reduce_scatter x2, waiting for transfers between devices, backward_layer(): lax.psum_scatter(jnp.dot(d_joined, up_flat.T, preferred_element_type=jnp....  62.7 us
    unnamed x196, local copies, waits for them, and re-layouts  51.6 us
    psum x1, blocking collectives, shards(): lax.psum((d_wqkv, d_wo, d_gain1, d_bias1, d_gain2, d_bias2), ('dp', 'tens...  41.8 us
  transfers between devices with their start and end apart: 16, of which 14 were waited for; matrix products, arithmetic and copies ran while one was open for 11% of the time, Pallas kernels for 0%

profile of v1, /device:TPU:0, one launch (start us, length us, event | category | flops | bytes accessed | tf_op | source)
XLA Modules:
  0.0 1190.1 jit_solution(2637360374122648278)
XLA Ops:
  12.0 4.2 convolution_convert_fusion.1
  17.3 5.0 fusion.103
  32.6 7.0 fusion.100
  41.5 57.2 %all-gather.3.cloned.1.call-done = bf16[2048,768]{1,0:T(8,128)(2,1)} async-done(((bf16[512,768]{1,0:T(8,128)(2,1)}), bf16[2048,768]{1,0:T(8,128)(2,1)}) %all-gather.3.cloned.1.call-update) | async-done | bytes 3145744 | tf_op jit(solution)/shard_map/all_gather | solution.py:105
  98.7 7.7 fusion.107
  113.2 3.9 convolution_convert_fusion.5
  117.9 58.3 %reduce-scatter.7.cloned.1.call-done = bf16[512,768]{1,0:T(8,128)(2,1)} async-done(((bf16[2048,768]{1,0:T(8,128)(2,1)}), bf16[512,768]{1,0:T(8,128)(2,1)}) %reduce-scatter.7.cloned.1.call-update) | async-done | bytes 786448 | tf_op jit(solution)/shard_map/reduce_scatter | solution.py:108
  178.2 4.1 convolution_convert_fusion
  187.7 5.0 fusion.105
  202.0 3.5 copy.112
  205.5 59.9 %all-gather.5.cloned.1.call-done = bf16[2048,768]{1,0:T(8,128)(2,1)} async-done(((bf16[512,768]{1,0:T(8,128)(2,1)}), bf16[2048,768]{1,0:T(8,128)(2,1)}) %all-gather.5.cloned.1.call-update) | async-done | bytes 3145744 | tf_op jit(solution)/shard_map/all_gather | solution.py:105
  265.5 7.7 fusion.108
  279.9 3.9 convolution_convert_fusion.4
  283.9 59.0 %reduce-scatter.9.cloned.1.call-done = bf16[512,768]{1,0:T(8,128)(2,1)} async-done(((bf16[2048,768]{1,0:T(8,128)(2,1)}), bf16[512,768]{1,0:T(8,128)(2,1)}) %reduce-scatter.9.cloned.1.call-update) | async-done | bytes 786448 | tf_op jit(solution)/shard_map/reduce_scatter | solution.py:108
  354.8 18.8 %collective-permute-done = bf16[512,768]{1,0:T(8,128)(2,1)} collective-permute-done((bf16[512,768]{1,0:T(8,128)(2,1)}, bf16[512,768]{1,0:T(8,128)(2,1)}, u32[]{:S(2)}, u32[]{:S(2)}) %collective-permute-start) | collective-permute-done | bytes 786464 | tf_op jit(solution)/shard_map/ppermute | solution.py:24
  373.6 14.2 %collective-permute-start.2 = (bf16[512,768]{1,0:T(8,128)(2,1)}, bf16[512,768]{1,0:T(8,128)(2,1)}, u32[]{:S(2)}, u32[]{:S(2)}) collective-permute-start(bf16[512,768]{1,0:T(8,128)(2,1)} %collective-permute-done), channel_id=1, source_target_pairs={{0,1},{1,2},{2,3},{3,0},{4,5},{5,6},{6,7},{7,4},{8,9},{9,10},{10,1... | collective-permute-start | bytes 2359304 | tf_op jit(solution)/shard_map/ppermute | solution.py:24
  392.1 13.8 %collective-permute-done.2 = bf16[512,768]{1,0:T(8,128)(2,1)} collective-permute-done((bf16[512,768]{1,0:T(8,128)(2,1)}, bf16[512,768]{1,0:T(8,128)(2,1)}, u32[]{:S(2)}, u32[]{:S(2)}) %collective-permute-start.2) | collective-permute-done | bytes 786464 | tf_op jit(solution)/shard_map/ppermute | solution.py:24
  408.0 12.6 %fusion.25 = (f32[2048,768]{1,0:T(8,128)S(1)}, f32[2048,768]{1,0:T(8,128)S(1)}) fusion(f32[2048,1536]{1,0:T(8,128)} %copy-done.9, bf16[2048,768]{1,0:T(8,128)(2,1)} %constant_dynamic-update-slice_fusion.3, bf16[2,768,768]{2,1,0:T(8,128)(2,1)S(1)} %copy-done.73), kind=kOutput, calls=%fused_computation.70 | convolution fusion | flops 2456813568 | bytes 29491200 | tf_op jit(solution)/shard_map/dot_general | solution.py:150
  425.1 6.4 convolution_convert_fusion.7
  431.7 59.2 %reduce-scatter.11.cloned.1.call-done = bf16[512,768]{1,0:T(8,128)(2,1)} async-done(((bf16[2048,768]{1,0:T(8,128)(2,1)}), bf16[512,768]{1,0:T(8,128)(2,1)}) %reduce-scatter.11.cloned.1.call-update) | async-done | bytes 786448 | tf_op jit(solution)/shard_map/reduce_scatter | solution.py:155
  497.3 7.7 fusion.51
  505.0 9.4 multiply_reduce_fusion.1
  514.4 6.9 multiply_convert_fusion.1
  534.7 18.5 %collective-permute-done.3 = bf16[512,768]{1,0:T(8,128)(2,1)S(1)} collective-permute-done((bf16[512,768]{1,0:T(8,128)(2,1)S(1)}, bf16[512,768]{1,0:T(8,128)(2,1)S(1)}, u32[]{:S(2)}, u32[]{:S(2)}) %collective-permute-start.3) | collective-permute-done | bytes 786464 | tf_op jit(solution)/shard_map/ppermute | solution.py:24
  553.2 14.0 %collective-permute-start.5 = (bf16[512,768]{1,0:T(8,128)(2,1)S(1)}, bf16[512,768]{1,0:T(8,128)(2,1)S(1)}, u32[]{:S(2)}, u32[]{:S(2)}) collective-permute-start(bf16[512,768]{1,0:T(8,128)(2,1)S(1)} %collective-permute-done.3), channel_id=1, source_target_pairs={{0,1},{1,2},{2,3},{3,0},{4,5},{5,6},{6,7},{7,4},{8,9},{9,10},{10,1... | collective-permute-start | bytes 2359304 | tf_op jit(solution)/shard_map/ppermute | solution.py:24
  568.8 16.7 %collective-permute-done.5 = bf16[512,768]{1,0:T(8,128)(2,1)S(1)} collective-permute-done((bf16[512,768]{1,0:T(8,128)(2,1)S(1)}, bf16[512,768]{1,0:T(8,128)(2,1)S(1)}, u32[]{:S(2)}, u32[]{:S(2)}) %collective-permute-start.5) | collective-permute-done | bytes 786464 | tf_op jit(solution)/shard_map/ppermute | solution.py:24
  585.7 11.9 %fusion.24 = (f32[2048,768]{1,0:T(8,128)}, f32[2048,768]{1,0:T(8,128)}) fusion(f32[2048,1536]{1,0:T(8,128)S(1)} %bitcast.154, bf16[2048,768]{1,0:T(8,128)(2,1)S(1)} %constant_dynamic-update-slice_fusion.7, bf16[2,768,768]{2,1,0:T(8,128)(2,1)} %param.20), kind=kOutput, calls=%fused_computation.69 | convolution fusion | flops 2456813568 | bytes 29491200 | tf_op jit(solution)/shard_map/dot_general | solution.py:150
  597.6 9.3 convolution_convert_fusion.6
  607.2 6.5 convolution_convert_fusion.8
  613.8 12.0 %convolution_convert_fusion.2 = bf16[768,1536]{1,0:T(8,128)(2,1)} fusion(bf16[2048,768]{1,0:T(8,128)(2,1)} %all-gather.5.cloned.1.call-done, f32[2048,768]{1,0:T(8,128)} %copy-done.82, f32[2048,768]{1,0:T(8,128)} %copy-done.81), kind=kOutput, calls=%fused_computation.50 | convolution fusion | flops 4839309312 | bytes 18087936 | tf_op jit(solution)/shard_map/dot_general | solution.py:154
  625.8 6.0 convert_element_type.181
  631.8 6.6 convolution_convert_fusion.9
  638.7 3.6 convolution_bitcast_fusion.2
  642.3 5.0 convolution_bitcast_fusion
  647.4 9.3 convolution_convert_fusion.3
  656.7 6.0 convert_element_type.179
  662.7 3.5 reduce-scatter.13.cloned.1.call-done
  674.1 10.9 multiply_reduce_fusion
  687.2 7.0 multiply_convert_fusion
  702.7 5.0 convolution_bitcast_fusion.1
  712.6 34.7 %reduce-scatter.15.cloned.1.call-done = bf16[768,96]{0,1:T(8,128)(2,1)} async-done(((bf16[768,768]{0,1:T(8,128)(2,1)}), bf16[768,96]{0,1:T(8,128)(2,1)}) %reduce-scatter.15.cloned.1.call-update) | async-done | bytes 147472 | tf_op jit(solution)/shard_map/reduce_scatter | solution.py:254
  749.1 88.5 %all-reduce.14.cloned.1.call-done = (bf16[768,2,768]{2,1,0:T(2,128)(2,1)}, bf16[768,2,768]{2,1,0:T(2,128)(2,1)}) async-done(((bf16[768,2,768]{2,1,0:T(2,128)(2,1)}, bf16[768,2,768]{2,1,0:T(2,128)(2,1)}), (bf16[768,2,768]{2,1,0:T(2,128)(2,1)}, bf16[768,2,768]{2,1,0:T(2,128)(2,1)})) %all-reduce.14.cloned.1.call-update) | async-done | bytes 4718608
  841.7 41.8 %all-reduce.6 = (f32[1,768]{1,0:T(1,128)S(1)}, f32[1,768]{1,0:T(1,128)S(1)}, f32[1,768]{1,0:T(1,128)S(1)}, f32[1,768]{1,0:T(1,128)S(1)}, f32[1,768]{1,0:T(1,128)...) all-reduce(f32[1,768]{1,0:T(1,128)S(1)} %stack.101, ...), channel_id=1, replica_groups=mesh['dp'=8,'tensor'=4] {'dp','tensor'}, use_global_device_ids=true, to_apply=%region_35.36 | all-reduce | flops 6144 | bytes 49152 | tf_op jit(solution)/shard_map/psum | solution.py:247
  885.9 5.5 add_add_fusion.4
  891.4 260.8 %all-reduce.12.cloned.1.call-done = (f32[1,768,2304]{1,2,0:T(8,128)}, f32[1,768,2304]{1,2,0:T(8,128)}, f32[1,768,768]{2,1,0:T(8,128)}, f32[1,768,768]{2,1,0:T(8,128)}) async-done(((f32[1,768,2304]{1,2,0:T(8,128)}, f32[1,768,2304]{1,2,0:T(8,128)}, f32[1,768,768]{2,1,0:T(8,128)}, f32[1,768,768]{2,1,0:T(8,128)}), (f32[1,768,2304]{1,2,0:T(8,128)}, f32[1,768,2304]{1,2,0:T(8,128)}, f32[1,768,768]{2,1,0:T(8,128)}, ...) | async-done | bytes 18874384 | tf_op jit(solution)/shard_map/psum | solution.py:247
  1152.2 11.0 pad_maximum_fusion
  1163.2 15.4 %copy.101 = f32[2,768,2304]{2,1,0:T(8,128)} copy(f32[2,768,2304]{1,2,0:T(8,128)} %pad_maximum_fusion) | data formatting | bytes 28311552
  1178.6 4.2 pad_maximum_fusion.1
  (323 shorter events, 123.4 us)
Async XLA Ops:
  7.2 91.5 %all-gather.3.cloned.1.call-start = ((), (), s32[]{:S(2)}) async-start(), calls=%async_computation.6 | async-start | bytes 3932160 | tf_op jit(solution)/shard_map/all_gather | solution.py:105
  17.3 7.0 copy-start.10
  30.0 146.3 %copy-start.2 = (f32[512,768]{1,0:T(8,128)}, f32[512,768]{1,0:T(8,128)S(1)}, u32[]{:S(2)}) copy-start(f32[512,768]{1,0:T(8,128)S(1)} %get-tuple-element.116) | copy-start | bytes 4718596
  30.0 146.2 %copy-start.54 = (f32[512]{0:T(512)}, f32[512]{0:T(512)S(1)}, u32[]{:S(2)}) copy-start(f32[512]{0:T(512)S(1)} %broadcast_multiply_fusion.3) | copy-start | bytes 6148
  31.1 145.1 %copy-start.56 = (f32[512]{0:T(512)}, f32[512]{0:T(512)S(1)}, u32[]{:S(2)}) copy-start(f32[512]{0:T(512)S(1)} %fusion.80) | copy-start | bytes 6148
  31.1 145.1 %copy-start.52 = (f32[768]{0:T(1024)}, f32[768]{0:T(1024)S(1)}, u32[]{:S(2)}) copy-start(f32[768]{0:T(1024)S(1)} %get-tuple-element.126) | copy-start | bytes 9220
  32.4 143.9 %reduce-scatter.7.cloned.1.call-start = ((), (), s32[]{:S(2)}) async-start(), calls=%async_computation.7 | async-start | bytes 3932160 | tf_op jit(solution)/shard_map/reduce_scatter | solution.py:108
  106.5 6.7 copy-start.71
  117.2 148.3 %all-gather.5.cloned.1.call-start = ((), (), s32[]{:S(2)}) async-start(), calls=%async_computation.8 | async-start | bytes 3932160 | tf_op jit(solution)/shard_map/all_gather | solution.py:105
  117.9 81.4 %copy-start.60 = (f32[768]{0:T(1024)}, f32[768]{0:T(1024)S(1)}, u32[]{:S(2)}) copy-start(f32[768]{0:T(1024)S(1)} %get-tuple-element.65) | copy-start | bytes 9220
  185.1 7.6 copy-start.16
  187.7 6.9 copy-start.12
  201.8 141.1 %reduce-scatter.9.cloned.1.call-start = ((), (), s32[]{:S(2)}) async-start(), calls=%async_computation.9 | async-start | bytes 3932160 | tf_op jit(solution)/shard_map/reduce_scatter | solution.py:108
  273.3 6.7 copy-start.72
  283.9 207.0 %reduce-scatter.11.cloned.1.call-start = ((), (), s32[]{:S(2)}) async-start(), calls=%async_computation.10 | async-start | bytes 3932160 | tf_op jit(solution)/shard_map/reduce_scatter | solution.py:155
  351.0 22.6 %collective-permute-start = (bf16[512,768]{1,0:T(8,128)(2,1)}, bf16[512,768]{1,0:T(8,128)(2,1)}, u32[]{:S(2)}, u32[]{:S(2)}) collective-permute-start(bf16[512,768]{1,0:T(8,128)(2,1)} %get-tuple-element.93), channel_id=1, source_target_pairs={{0,1},{1,2},{2,3},{3,0},{4,5},{5,6},{6,7},{7,4},{8,9},{9,10},{10,1... | collective-permute-start | bytes 2359304 | tf_op jit(solution)/shard_map/ppermute | solution.py:24
  351.9 38.1 %collective-permute-start.1 = (bf16[512,768]{1,0:T(8,128)(2,1)}, bf16[512,768]{1,0:T(8,128)(2,1)}, u32[]{:S(2)}, u32[]{:S(2)}) collective-permute-start(bf16[512,768]{1,0:T(8,128)(2,1)} %get-tuple-element.93), channel_id=1, source_target_pairs={{0,3},{1,0},{2,1},{3,2},{4,7},{5,4},{6,5},{7,6},{8,11},{9,8},{10,9... | collective-permute-start | bytes 2359304 | tf_op jit(solution)/shard_map/ppermute | solution.py:29
  373.6 32.3 %collective-permute-start.2 = (bf16[512,768]{1,0:T(8,128)(2,1)}, bf16[512,768]{1,0:T(8,128)(2,1)}, u32[]{:S(2)}, u32[]{:S(2)}) collective-permute-start(bf16[512,768]{1,0:T(8,128)(2,1)} %collective-permute-done), channel_id=1, source_target_pairs={{0,1},{1,2},{2,3},{3,0},{4,5},{5,6},{6,7},{7,4},{8,9},{9,10},{10,1... | collective-permute-start | bytes 2359304 | tf_op jit(solution)/shard_map/ppermute | solution.py:24
  387.8 20.2 %copy-start.73 = (bf16[2,768,768]{2,1,0:T(8,128)(2,1)S(1)}, bf16[2,768,768]{2,1,0:T(8,128)(2,1)}, u32[]{:S(2)}) copy-start(bf16[2,768,768]{2,1,0:T(8,128)(2,1)} %param.20) | copy-start | bytes 7077892
  408.0 17.2 %copy-start.41 = (bf16[96,8,2,768]{3,1,2,0:T(8,128)(2,1)S(1)}, bf16[96,8,2,768]{3,1,2,0:T(8,128)(2,1)}, u32[]{:S(2)}) copy-start(bf16[96,8,2,768]{3,1,2,0:T(8,128)(2,1)} %copy.112) | copy-start | bytes 7077892
  431.6 234.6 %reduce-scatter.13.cloned.1.call-start = ((), (), s32[]{:S(2)}) async-start(), calls=%async_computation.11 | async-start | bytes 3932160 | tf_op jit(solution)/shard_map/reduce_scatter | solution.py:155
  497.3 7.7 copy-start.13
  497.3 17.1 %slice-start.3 = ((s8[12582912]{0:T(1024)(128)(4,1)}), s8[4194304]{0:T(1024)(128)(4,1)S(1)}, s32[]{:S(2)}) async-start(s8[12582912]{0:T(1024)(128)(4,1)} %bitcast.151), calls=%async_computation.19 | async-start | bytes 8388608
  497.3 17.1 %slice-start.4 = ((s8[12582912]{0:T(1024)(128)(4,1)}), s8[4194304]{0:T(1024)(128)(4,1)S(1)}, s32[]{:S(2)}) async-start(s8[12582912]{0:T(1024)(128)(4,1)} %bitcast.151), calls=%async_computation.20 | async-start | bytes 8388608
  505.0 9.4 slice-start.5
  514.4 6.9 copy-start.35
  526.5 59.1 %slice-start.6 = ((s8[12582912]{0:T(1024)(128)(4,1)}), s8[4194304]{0:T(1024)(128)(4,1)S(1)}, s32[]{:S(2)}) async-start(s8[12582912]{0:T(1024)(128)(4,1)} %bitcast.153), calls=%async_computation.22 | async-start | bytes 8388608
  526.5 59.1 %slice-start.7 = ((s8[12582912]{0:T(1024)(128)(4,1)}), s8[4194304]{0:T(1024)(128)(4,1)S(1)}, s32[]{:S(2)}) async-start(s8[12582912]{0:T(1024)(128)(4,1)} %bitcast.153), calls=%async_computation.23 | async-start | bytes 8388608
  529.1 56.5 %slice-start.8 = ((s8[12582912]{0:T(1024)(128)(4,1)}), s8[4194304]{0:T(1024)(128)(4,1)S(1)}, s32[]{:S(2)}) async-start(s8[12582912]{0:T(1024)(128)(4,1)} %bitcast.153), calls=%async_computation.24 | async-start | bytes 8388608
  530.9 22.3 %collective-permute-start.3 = (bf16[512,768]{1,0:T(8,128)(2,1)S(1)}, bf16[512,768]{1,0:T(8,128)(2,1)S(1)}, u32[]{:S(2)}, u32[]{:S(2)}) collective-permute-start(bf16[512,768]{1,0:T(8,128)(2,1)S(1)} %get-tuple-element.87), channel_id=1, source_target_pairs={{0,1},{1,2},{2,3},{3,0},{4,5},{5,6},{6,7},{7,4},{8,9},{9,10},{10,1... | collective-permute-start | bytes 2359304 | tf_op jit(solution)/shard_map/ppermute | solution.py:24
  531.9 36.9 %collective-permute-start.4 = (bf16[512,768]{1,0:T(8,128)(2,1)S(1)}, bf16[512,768]{1,0:T(8,128)(2,1)S(1)}, u32[]{:S(2)}, u32[]{:S(2)}) collective-permute-start(bf16[512,768]{1,0:T(8,128)(2,1)S(1)} %get-tuple-element.87), channel_id=1, source_target_pairs={{0,3},{1,0},{2,1},{3,2},{4,7},{5,4},{6,5},{7,6},{8,11},{9,8},{10,9... | collective-permute-start | bytes 2359304 | tf_op jit(solution)/shard_map/ppermute | solution.py:29
  553.2 32.4 %collective-permute-start.5 = (bf16[512,768]{1,0:T(8,128)(2,1)S(1)}, bf16[512,768]{1,0:T(8,128)(2,1)S(1)}, u32[]{:S(2)}, u32[]{:S(2)}) collective-permute-start(bf16[512,768]{1,0:T(8,128)(2,1)S(1)} %collective-permute-done.3), channel_id=1, source_target_pairs={{0,1},{1,2},{2,3},{3,0},{4,5},{5,6},{6,7},{7,4},{8,9},{9,10},{10,1... | collective-permute-start | bytes 2359304 | tf_op jit(solution)/shard_map/ppermute | solution.py:24
  585.7 12.0 %copy-start.24 = (bf16[2048,768]{1,0:T(8,128)(2,1)}, bf16[2048,768]{1,0:T(8,128)(2,1)S(1)}, u32[]{:S(2)}) copy-start(bf16[2048,768]{1,0:T(8,128)(2,1)S(1)} %constant_dynamic-update-slice_fusion.7) | copy-start | bytes 9437188
  585.7 12.0 %copy-start.40 = (bf16[96,8,2,768]{3,1,2,0:T(8,128)(2,1)S(1)}, bf16[96,8,2,768]{3,1,2,0:T(8,128)(2,1)}, u32[]{:S(2)}) copy-start(bf16[96,8,2,768]{3,1,2,0:T(8,128)(2,1)} %copy.111) | copy-start | bytes 7077892
  607.0 105.6 %reduce-scatter.17.cloned.1.call-start = ((), (), s32[]{:S(2)}) async-start(), calls=%async_computation.13 | async-start | bytes 1327104 | tf_op jit(solution)/shard_map/reduce_scatter | solution.py:254
  613.7 133.5 %reduce-scatter.15.cloned.1.call-start = ((), (), s32[]{:S(2)}) async-start(), calls=%async_computation.12 | async-start | bytes 1327104 | tf_op jit(solution)/shard_map/reduce_scatter | solution.py:254
  638.4 199.2 %all-reduce.14.cloned.1.call-start = ((), (), s32[]{:S(2)}) async-start(), calls=%async_computation.15 | async-start | bytes 9437184
  638.7 8.7 slice-start.11
  662.7 489.5 %all-reduce.12.cloned.1.call-start = ((), (), s32[]{:S(2)}) async-start(), calls=%async_computation.14 | async-start | bytes 37748736 | tf_op jit(solution)/shard_map/psum | solution.py:247
  674.1 11.0 slice-start
  674.1 11.7 slice-start.1
  674.1 13.1 %slice-start.2 = ((s8[12582912]{0:T(1024)(128)(4,1)}), s8[4194304]{0:T(1024)(128)(4,1)S(1)}, s32[]{:S(2)}) async-start(s8[12582912]{0:T(1024)(128)(4,1)} %bitcast.149), calls=%async_computation.18 | async-start | bytes 8388608
  687.2 7.0 copy-start.19
  687.2 7.0 copy-start.27
  709.9 176.1 %copy-start.20 = (f32[512,768]{1,0:T(8,128)S(1)}, f32[512,768]{1,0:T(8,128)}, u32[]{:S(2)}) copy-start(f32[512,768]{1,0:T(8,128)} %copy-done.18) | copy-start | bytes 4718596
  709.9 176.1 %copy-start.37 = (bf16[12,64,512]{2,1,0:T(8,128)(2,1)S(1)}, bf16[12,64,512]{2,1,0:T(8,128)(2,1)}, u32[]{:S(2)}) copy-start(bf16[12,64,512]{2,1,0:T(8,128)(2,1)} %copy-done.36) | copy-start | bytes 2359300
  709.9 176.0 %copy-start.48 = (bf16[12,64,512]{2,1,0:T(8,128)(2,1)S(1)}, bf16[12,64,512]{2,1,0:T(8,128)(2,1)}, u32[]{:S(2)}) copy-start(bf16[12,64,512]{2,1,0:T(8,128)(2,1)} %copy-done.47) | copy-start | bytes 2359300
  1163.2 15.4 %copy-start.42 = (f32[1,768,768]{2,1,0:T(8,128)S(1)}, f32[1,768,768]{2,1,0:T(8,128)}, u32[]{:S(2)}) copy-start(f32[1,768,768]{2,1,0:T(8,128)} %get-tuple-element.80) | copy-start | bytes 7077892
  (64 other events, 185.4 us)
Sparse Core Ops, SparseCore 0:
  32.5 66.1 all-gather.2
  117.3 58.8 reduce-scatter.6
  201.9 63.5 all-gather.4
  284.0 58.8 reduce-scatter.8
  431.7 59.0 reduce-scatter.10
  607.1 59.1 reduce-scatter.12
  670.0 36.7 reduce-scatter.16
  710.4 36.7 reduce-scatter.14
  750.6 86.9 all-reduce.13
  845.6 306.5 all-reduce.11
